TPU v7x, 32 devices: a whole 2x2x4 slice. The times are simulated.
32 devices in a mesh: vec: 4 (over y, x), orb: 8 (over z, core).
Axes of the slice: x: 2, y: 2, z: 4, core: 2. Of those that a mesh axis runs over, the one named last changes fastest.
Arguments:
- chol_occ: float32 [44, 96, 1056], P('vec', 'orb'), may hold values from -6 to 6
- chol_vir: float32 [44, 960, 1056], P('vec', 'orb'), may hold values from -6 to 6
- singles: float32 [96, 960], P('orb'), may hold values from -0.6 to 0.6
Outputs:
- dressed_vir: float32 [44, 960, 1056], P('vec', 'orb')
- dressed_ov: float32 [44, 96, 960], P(None, 'orb', 'vec')
- fock_ov: float32 [96, 960], P('orb')
All inputs are finite; a program needn't handle non-finite values.
Results may differ from a plain program's by a relative error of at most 0.000086.
Values sent between devices are 32-bit elements; how exact they have to be, the bound alone decides.
A program may use at most 64 MiB of HBM per device.

v0:
```python
import jax
import jax.numpy as jnp
from jax import lax
from jax.sharding import PartitionSpec as P


def dress_right(matrix_rows, amplitudes):
    occ_width = amplitudes.shape[0]
    occ_cols = matrix_rows[:, :, :occ_width]
    extra_term = jnp.einsum("qrj,ja->qra", occ_cols, amplitudes, precision=lax.Precision.HIGHEST)
    return jnp.concatenate([occ_cols, matrix_rows[:, :, occ_width:] + extra_term], axis=2)


def dress_left(vir_rows, occ_all, amp_cols):
    return vir_rows - jnp.einsum("qin,ia->qan", occ_all, amp_cols, precision=lax.Precision.HIGHEST)


def shards(chol_occ, chol_vir, singles):
    amplitudes = lax.all_gather(singles, "orb", axis=0, tiled=True)
    occ_width = amplitudes.shape[0]
    vir_local = chol_vir.shape[1]
    vir_start = lax.axis_index("orb") * vir_local
    amp_cols = lax.dynamic_slice_in_dim(amplitudes, vir_start, vir_local, 1)
    occ_all = lax.all_gather(chol_occ, "orb", axis=1, tiled=True)
    dressed_vir = dress_right(dress_left(chol_vir, occ_all, amp_cols), amplitudes)
    dressed_occ = dress_right(chol_occ, amplitudes)
    local_rows = chol_occ.shape[1]
    first_row = lax.axis_index("orb") * local_rows
    row_ids = lax.broadcasted_iota(jnp.int32, (local_rows, chol_occ.shape[2]), 0) + first_row
    col_ids = lax.broadcasted_iota(jnp.int32, (local_rows, chol_occ.shape[2]), 1)
    diag_mask = jnp.where(row_ids == col_ids, 1.0, 0.0).astype(jnp.float32)
    traces_local = jnp.sum(chol_occ * diag_mask[None], axis=(1, 2))
    traces = lax.psum(traces_local, "orb")
    ov_block = dressed_occ[:, :, occ_width:]
    total_vectors = chol_occ.shape[0] * lax.axis_size("vec")
    fock_part = (
        jnp.einsum("q,qia->ia", traces, ov_block, precision=lax.Precision.HIGHEST) / total_vectors
    )
    fock_ov = lax.psum(fock_part, "vec")
    pair_blocks = lax.all_to_all(ov_block, "vec", split_axis=2, concat_axis=0, tiled=True)
    return (dressed_vir, pair_blocks, fock_ov)


def solution(mesh):
    return jax.shard_map(
        shards,
        mesh=mesh,
        in_specs=(P("vec", "orb", None), P("vec", "orb", None), P("orb", None)),
        out_specs=(P("vec", "orb", None), P(None, "orb", "vec"), P("orb", None)),
        check_vma=False,
    )
```

profile of v0, /device:TPU:0, one launch (start us, length us, event | category | flops | bytes accessed | tf_op | source)
XLA Modules:
  0.0 127.6 jit_solution(5254257879419233849)
XLA Ops:
  7.2 0.0 all-gather.3.cloned.1.call-start
  7.2 2.3 %copy.10 = f32[11,12,1056]{2,0,1:T(8,128)} copy(f32[11,12,1056]{2,1,0:T(8,128)} %param.3) | data formatting | bytes 1115136 | tf_op args[0]
  9.5 0.0 all-gather.3.cloned.1.call-update
  9.5 16.7 %all-gather = f32[8,12,960]{2,1,0:T(8,128)S(1)} all-gather(f32[1,12,960]{2,1,0:T(8,128)} %bitcast.22), channel_id=1, replica_groups=mesh['vec'=4,'orb'=8] {'orb'}, dimensions={0}, use_global_device_ids=true | all-gather | bytes 414720 | tf_op jit(solution)/shard_map/all_gather | solution.py:19
  26.3 1.9 %convolution_add_fusion = f32[11,12,960]{2,1,0:T(8,128)S(1)} fusion(f32[96,960,1]{1,0,2:T(8,128)S(1)} %reshape.23, f32[11,12,1056]{2,1,0:T(8,128)} %param.3), kind=kOutput, calls=%fused_computation.4 | convolution fusion | flops 146108160 | bytes 1433088 | tf_op jit(solution)/shard_map/qrj,ja->qra/dot_general | solution.py:10
  28.2 6.0 %copy.13 = f32[11,12,960]{1,0,2:T(8,128)} copy(f32[11,12,960]{2,1,0:T(8,128)S(1)} %convolution_add_fusion) | data formatting | bytes 1013760 | tf_op jit(solution)/shard_map/add | solution.py:11
  34.2 0.0 copy-start
  34.2 6.5 %reshape.27 = f32[4,1,31680]{2,1,0:T(1,128)} reshape(f32[960,11,12]{2,1,0:T(8,128)} %bitcast.20) | data formatting | bytes 1013760
  40.7 0.1 fusion.4
  40.8 0.0 copy-done
  40.8 0.2 multiply_reduce_fusion
  41.0 3.7 %all-to-all-start = ((f32[4,1,31680]{2,1,0:T(1,128)}), f32[4,1,31680]{2,1,0:T(1,128)S(1)}, u32[]{:S(2)}, u32[]{:S(2)}) async-start(f32[4,1,31680]{2,1,0:T(1,128)} %reshape.27), calls=%async_computation | async-start | bytes 1015808 | tf_op jit(solution)/shard_map/all_to_all | solution.py:40
  44.7 19.3 %psum.14 = f32[11]{0:T(128)S(1)} all-reduce(f32[11]{0:T(128)S(1)} %multiply_reduce_fusion), channel_id=1, replica_groups=mesh['vec'=4,'orb'=8] {'orb'}, use_global_device_ids=true, to_apply=%region_1.2 | all-reduce | flops 11 | bytes 88 | tf_op jit(solution)/shard_map/psum | solution.py:33
  64.0 0.8 fusion.1
  64.9 17.7 %psum.15 = f32[12,960]{1,0:T(8,128)} all-reduce(f32[12,960]{1,0:T(8,128)S(1)} %bitcast_multiply_fusion), channel_id=1, replica_groups=mesh['vec'=4,'orb'=8] {'vec'}, use_global_device_ids=true, to_apply=%region_2.3 | all-reduce | flops 11520 | bytes 92160 | tf_op jit(solution)/shard_map/psum | solution.py:39
  82.5 0.0 all-to-all-done
  82.5 0.5 broadcast.18
  83.0 2.1 %reduce = f32[4,31680]{1,0:T(4,128)S(1)} reduce(f32[4,1,31680]{2,1,0:T(1,128)S(1)} %all-to-all-done, f32[]{:T(128)} %broadcast.18), dimensions={1}, to_apply=%all_to_all.13.reduce_sub_computation | reduce | bytes 1013764 | tf_op jit(solution)/shard_map/all_to_all | solution.py:40
  85.2 6.0 %reshape.28 = f32[960,11,12]{2,1,0:T(8,128)} reshape(f32[4,31680]{1,0:T(4,128)S(1)} %reduce) | data formatting | bytes 1013760
  91.2 6.2 %copy.14 = f32[11,12,4,240]{3,0,2,1:T(8,128)S(1)} copy(f32[11,12,4,240]{1,0,3,2:T(8,128)} %bitcast.19) | data formatting | bytes 1013760 | tf_op jit(solution)/shard_map/all_to_all | solution.py:40
  97.4 0.9 all_to_all.16
  98.3 0.0 all-gather.3.cloned.1.call-done
  98.3 14.5 %bitcast_subtract_fusion = f32[11,120,1056]{1,2,0:T(8,128)S(1)} fusion(f32[11,120,1056]{1,2,0:T(8,128)} %param.4, f32[11,96,1056]{2,0,1:T(8,128)} %all-gather.3.cloned.1.call-done, f32[96,960]{1,0:T(8,128)S(1)} %reshape.21, s32[]{:T(128)S(6)} %select_n.11), kind=kOutput, calls=%fused_computation.1 | convolution fusion | flops 1607189760 | bytes 15661060 | tf_op jit(solution)/shard_map/qin,ia->qan/dot_general | solution.py:15
  112.9 4.7 %slice_add_fusion = f32[11,120,960]{1,2,0:T(8,128)S(1)} fusion(f32[11,120,1056]{1,2,0:T(8,128)S(1)} %bitcast_subtract_fusion, f32[96,960,1]{1,0,2:T(8,128)S(1)} %reshape.23), kind=kOutput, calls=%fused_computation.2 | convolution fusion | flops 1461081600 | bytes 11013120 | tf_op jit(solution)/shard_map/qrj,ja->qra/dot_general | solution.py:10
  117.6 3.2 %pad_maximum_fusion = f32[11,120,1056]{1,2,0:T(8,128)} fusion(f32[11,120,960]{1,2,0:T(8,128)S(1)} %slice_add_fusion, f32[11,120,96]{1,2,0:T(8,128)S(1)} %slice.16), kind=kLoop, calls=%fused_computation | loop fusion | flops 1393920 | bytes 11151360 | tf_op jit(solution)/shard_map/concatenate | solution.py:11
  (5 shorter events, 0.1 us)
Async XLA Ops:
  7.2 91.1 %all-gather.3.cloned.1.call-start = ((), (), s32[]{:S(2)}) async-start(), calls=%async_computation.1 | async-start | bytes 7962624 | tf_op jit(solution)/shard_map/all_gather | solution.py:24
  34.2 6.6 %copy-start = (f32[11,12,1056]{2,1,0:T(8,128)S(1)}, f32[11,12,1056]{2,1,0:T(8,128)}, u32[]{:S(2)}) copy-start(f32[11,12,1056]{2,1,0:T(8,128)} %param.3) | copy-start | bytes 1672708
  41.0 41.6 %all-to-all-start = ((f32[4,1,31680]{2,1,0:T(1,128)}), f32[4,1,31680]{2,1,0:T(1,128)S(1)}, u32[]{:S(2)}, u32[]{:S(2)}) async-start(f32[4,1,31680]{2,1,0:T(1,128)} %reshape.27), calls=%async_computation | async-start | bytes 1015808 | tf_op jit(solution)/shard_map/all_to_all | solution.py:40
Sparse Core Ops, SparseCore 0:
  10.2 74.4 all-gather.2
where the time goes:
time: 128 us
  blocking collectives  53.7 us (42%)
  local copies, waits for them, and re-layouts  28.5 us (22%)
  matrix products  22 us (17%)
  between operations  14.1 us (11%)
  other arithmetic  5.58 us (4%)
  starting transfers between devices  3.76 us (3%)
    psum x1, blocking collectives, shards(): traces = lax.psum(traces_local, 'orb')  19.3 us
    psum x1, blocking collectives, shards(): fock_ov = lax.psum(fock_part, 'vec')  17.7 us
    all_gather x1, blocking collectives, shards(): amplitudes = lax.all_gather(singles, 'orb', axis=0, tiled=True)  16.7 us
    unnamed x7, local copies, waits for them, and re-layouts  14.9 us
    dot_general x1, matrix products, dress_left(): jnp.einsum('qin,ia->qan', occ_all, amp_cols, precision=lax.Precision.HIGH...  14.5 us
    all_to_all x3, local copies, waits for them, and re-layouts, shards(): lax.all_to_all(ov_block, 'vec', split_axis=2, concat_axis=0, tiled=True)  7.57 us
    dot_general x2, matrix products, dress_right(): jnp.einsum('qrj,ja->qra', occ_cols, amplitudes, precision=lax.Precision.H...  6.66 us
    add x1, local copies, waits for them, and re-layouts, dress_right(): matrix_rows[:, :, occ_width:] + extra_term  5.96 us
  transfers between devices with their start and end apart: 2, of which 0 were waited for; matrix products, arithmetic and copies ran while one was open for 24% of the time, Pallas kernels for 0%

commit v1 on v0

--- a/solution.py
+++ b/solution.py
@@ -2,6 +2,18 @@
 import jax.numpy as jnp
 from jax import lax
 from jax.sharding import PartitionSpec as P
+
+
+def rotated_exchange(x, axis, split, join):
+    ways, here = (lax.axis_size(axis), lax.axis_index(axis))
+    width = x.shape[split] // ways
+    turned = jnp.roll(x, -here * width, axis=split)
+    got = [lax.slice_in_dim(turned, 0, width, axis=split)]
+    for far in range(1, ways):
+        sent = lax.slice_in_dim(turned, far * width, (far + 1) * width, axis=split)
+        got.append(lax.ppermute(sent, axis, [(d, (d + far) % ways) for d in range(ways)]))
+    line = jnp.concatenate(got[::-1], axis=join)
+    return jnp.roll(line, (here + 1) * got[0].shape[join], axis=join)
 
 
 def dress_right(matrix_rows, amplitudes):
@@ -37,7 +49,7 @@
         jnp.einsum("q,qia->ia", traces, ov_block, precision=lax.Precision.HIGHEST) / total_vectors
     )
     fock_ov = lax.psum(fock_part, "vec")
-    pair_blocks = lax.all_to_all(ov_block, "vec", split_axis=2, concat_axis=0, tiled=True)
+    pair_blocks = rotated_exchange(ov_block, "vec", 2, 0)
     return (dressed_vir, pair_blocks, fock_ov)
 
 

time: 128 us -> 114 us (0.89)
  local copies, waits for them, and re-layouts: 28.5 us -> 4.7 us
  waiting for transfers between devices: 0.02 us -> 14 us
  other arithmetic: 5.58 us -> 3.92 us
  matrix products: 22 us -> 20.6 us
    all_gather x1, waiting for transfers between devices: 0.01 us -> 13.9 us  [shards(): occ_all = lax.all_gather(chol_occ, 'orb', axis=1, tiled=True)]
    unnamed x7 -> x15, local copies, waits for them, and re-layouts: 14.9 us -> 3.61 us
    all_to_all x3 -> x0, local copies, waits for them, and re-layouts: 7.57 us -> none  [shards(): lax.all_to_all(ov_block, 'vec', split_axis=2, concat_axis=0, tiled=True)]
    add x1 -> x0, local copies, waits for them, and re-layouts: 5.96 us -> none  [dress_right(): matrix_rows[:, :, occ_width:] + extra_term]
    all_to_all x1 -> x0, starting transfers between devices: 3.72 us -> none  [shards(): lax.all_to_all(ov_block, 'vec', split_axis=2, concat_axis=0, tiled=True)]
    ppermute x0 -> x3, starting transfers between devices: none -> 3.49 us  [rotated_exchange(): lax.ppermute(sent, axis, [(d, (d + far) % ways) for d in range(ways)])]
    all_to_all x1 -> x0, other arithmetic: 2.12 us -> none  [shards(): lax.all_to_all(ov_block, 'vec', split_axis=2, concat_axis=0, tiled=True)]
  transfers between devices with their start and end apart: 2 -> 4, of which waited for: 0 -> 1; matrix products, arithmetic and copies ran while one was open for 24% -> 4% of each run, Pallas kernels for 0% -> 0%
where the time goes in v1:
time: 114 us
  blocking collectives  52.9 us (46%)
  matrix products  20.6 us (18%)
  between operations  14.3 us (13%)
  waiting for transfers between devices  14 us (12%)
  local copies, waits for them, and re-layouts  4.7 us (4%)
  other arithmetic  3.92 us (3%)
  starting transfers between devices  3.53 us (3%)
    psum x1, blocking collectives, shards(): traces = lax.psum(traces_local, 'orb')  18.6 us
    psum x1, blocking collectives, shards(): fock_ov = lax.psum(fock_part, 'vec')  17.5 us
    all_gather x1, blocking collectives, shards(): amplitudes = lax.all_gather(singles, 'orb', axis=0, tiled=True)  16.7 us
    dot_general x1, matrix products, dress_left(): jnp.einsum('qin,ia->qan', occ_all, amp_cols, precision=lax.Precision.HIGH...  14.3 us
    all_gather x1, waiting for transfers between devices, shards(): occ_all = lax.all_gather(chol_occ, 'orb', axis=1, tiled=True)  13.9 us
    dot_general x2, matrix products, dress_right(): jnp.einsum('qrj,ja->qra', occ_cols, amplitudes, precision=lax.Precision.H...  5.46 us
    unnamed x15, local copies, waits for them, and re-layouts  3.61 us
    ppermute x3, starting transfers between devices, rotated_exchange(): lax.ppermute(sent, axis, [(d, (d + far) % ways) for d in range(ways)])  3.49 us
  transfers between devices with their start and end apart: 4, of which 1 were waited for; matrix products, arithmetic and copies ran while one was open for 4% of the time, Pallas kernels for 0%

profile of v1, /device:TPU:0, one launch (start us, length us, event | category | flops | bytes accessed | tf_op | source)
XLA Modules:
  0.0 113.8 jit_solution(10011405049514472887)
XLA Ops:
  7.2 0.0 copy-start.1
  7.2 0.0 all-gather.3.cloned.1.call-start
  7.2 2.3 %copy.10 = f32[11,12,1056]{2,0,1:T(8,128)} copy(f32[11,12,1056]{2,1,0:T(8,128)} %param.3) | data formatting | bytes 1115136 | tf_op args[0]
  9.5 0.0 copy-start
  9.5 0.0 all-gather.3.cloned.1.call-update
  9.5 0.0 copy-done.1
  9.6 16.7 %all-gather = f32[8,12,960]{2,1,0:T(8,128)S(1)} all-gather(f32[1,12,960]{2,1,0:T(8,128)S(1)} %bitcast.13), channel_id=1, replica_groups=mesh['vec'=4,'orb'=8] {'orb'}, dimensions={0}, use_global_device_ids=true | all-gather | bytes 414720 | tf_op jit(solution)/shard_map/all_gather | solution.py:31
  26.4 0.0 copy-done
  26.4 0.7 convolution_add_fusion
  27.1 0.5 fusion.3
  27.6 1.0 fusion.11
  28.6 2.4 %collective-permute-start = (f32[11,12,240]{2,1,0:T(8,128)}, f32[11,12,240]{2,1,0:T(8,128)S(1)}, u32[]{:S(2)}, u32[]{:S(2)}) collective-permute-start(f32[11,12,240]{2,1,0:T(8,128)} %get-tuple-element.14), channel_id=1, source_target_pairs={{0,24},{8,0},{16,8},{24,16},{1,25},{9,1},{17,9},{25,17},{2,26},{10... | collective-permute-start | bytes 380168 | tf_op jit(solution)/shard_map/ppermute | solution.py:14
  30.9 0.6 collective-permute-start.1
  31.5 0.1 fusion.5
  31.6 0.2 multiply_reduce_fusion
  31.8 0.5 collective-permute-start.2
  32.3 18.6 %psum.14 = f32[11]{0:T(128)S(1)} all-reduce(f32[11]{0:T(128)S(1)} %multiply_reduce_fusion), channel_id=1, replica_groups=mesh['vec'=4,'orb'=8] {'orb'}, use_global_device_ids=true, to_apply=%region_1.2 | all-reduce | flops 11 | bytes 88 | tf_op jit(solution)/shard_map/psum | solution.py:45
  51.0 0.8 fusion.1
  51.8 17.5 %psum.15 = f32[12,960]{1,0:T(8,128)} all-reduce(f32[12,960]{1,0:T(8,128)S(1)} %bitcast_multiply_fusion), channel_id=1, replica_groups=mesh['vec'=4,'orb'=8] {'vec'}, use_global_device_ids=true, to_apply=%region_2.3 | all-reduce | flops 11520 | bytes 92160 | tf_op jit(solution)/shard_map/psum | solution.py:51
  69.4 0.0 collective-permute-done
  69.4 0.0 collective-permute-done.1
  69.4 0.0 collective-permute-done.2
  69.6 0.1 constant_dynamic-slice_fusion
  69.6 1.1 copy.13
  70.8 13.9 %all-gather.3.cloned.1.call-done = f32[11,96,1056]{2,0,1:T(8,128)} async-done(((f32[11,12,1056]{2,0,1:T(8,128)}), f32[11,96,1056]{2,0,1:T(8,128)}) %all-gather.3.cloned.1.call-update) | async-done | bytes 4460560 | tf_op jit(solution)/shard_map/all_gather | solution.py:36
  84.7 14.3 %bitcast_subtract_fusion = f32[11,120,1056]{1,2,0:T(8,128)S(1)} fusion(f32[11,120,1056]{1,2,0:T(8,128)} %param.4, f32[11,96,1056]{2,0,1:T(8,128)} %all-gather.3.cloned.1.call-done, f32[96,960]{1,0:T(8,128)S(1)} %reshape.21, s32[]{:T(128)S(6)} %select_n.34), kind=kOutput, calls=%fused_computation.1 | convolution fusion | flops 1607189760 | bytes 15661060 | tf_op jit(solution)/shard_map/qin,ia->qan/dot_general | solution.py:27
  99.0 4.7 %slice_add_fusion = f32[11,120,960]{1,2,0:T(8,128)S(1)} fusion(f32[11,120,1056]{1,2,0:T(8,128)S(1)} %bitcast_subtract_fusion, f32[96,960,1]{1,0,2:T(8,128)S(1)} %reshape.23), kind=kOutput, calls=%fused_computation.2 | convolution fusion | flops 1461081600 | bytes 11013120 | tf_op jit(solution)/shard_map/qrj,ja->qra/dot_general | solution.py:22
  103.8 3.2 %pad_maximum_fusion = f32[11,120,1056]{1,2,0:T(8,128)} fusion(f32[11,120,960]{1,2,0:T(8,128)S(1)} %slice_add_fusion, f32[11,120,96]{1,2,0:T(8,128)S(1)} %slice.32), kind=kLoop, calls=%fused_computation | loop fusion | flops 1393920 | bytes 11151360 | tf_op jit(solution)/shard_map/concatenate | solution.py:23
  (13 shorter events, 0.3 us)
Async XLA Ops:
  7.2 2.4 %copy-start.1 = (f32[12,960]{1,0:T(8,128)S(1)}, f32[12,960]{1,0:T(8,128)}, u32[]{:S(2)}) copy-start(f32[12,960]{1,0:T(8,128)} %param.5) | copy-start | bytes 138244
  7.2 77.5 %all-gather.3.cloned.1.call-start = ((), (), s32[]{:S(2)}) async-start(), calls=%async_computation | async-start | bytes 7962624 | tf_op jit(solution)/shard_map/all_gather | solution.py:36
  9.5 16.9 %copy-start = (f32[11,12,1056]{2,1,0:T(8,128)S(1)}, f32[11,12,1056]{2,1,0:T(8,128)}, u32[]{:S(2)}) copy-start(f32[11,12,1056]{2,1,0:T(8,128)} %param.3) | copy-start | bytes 1672708
  28.6 40.8 %collective-permute-start = (f32[11,12,240]{2,1,0:T(8,128)}, f32[11,12,240]{2,1,0:T(8,128)S(1)}, u32[]{:S(2)}, u32[]{:S(2)}) collective-permute-start(f32[11,12,240]{2,1,0:T(8,128)} %get-tuple-element.14), channel_id=1, source_target_pairs={{0,24},{8,0},{16,8},{24,16},{1,25},{9,1},{17,9},{25,17},{2,26},{10... | collective-permute-start | bytes 380168 | tf_op jit(solution)/shard_map/ppermute | solution.py:14
  30.9 38.5 %collective-permute-start.1 = (f32[11,12,240]{2,1,0:T(8,128)}, f32[11,12,240]{2,1,0:T(8,128)S(1)}, u32[]{:S(2)}, u32[]{:S(2)}) collective-permute-start(f32[11,12,240]{2,1,0:T(8,128)} %get-tuple-element.13), channel_id=1, source_target_pairs={{0,16},{8,24},{16,0},{24,8},{1,17},{9,25},{17,1},{25,9},{2,18},{10... | collective-permute-start | bytes 380168 | tf_op jit(solution)/shard_map/ppermute | solution.py:14
  31.8 37.7 %collective-permute-start.2 = (f32[11,12,240]{2,1,0:T(8,128)}, f32[11,12,240]{2,1,0:T(8,128)S(1)}, u32[]{:S(2)}, u32[]{:S(2)}) collective-permute-start(f32[11,12,240]{2,1,0:T(8,128)} %get-tuple-element.12), channel_id=1, source_target_pairs={{0,8},{8,16},{16,24},{24,0},{1,9},{9,17},{17,25},{25,1},{2,10},{10... | collective-permute-start | bytes 380168 | tf_op jit(solution)/shard_map/ppermute | solution.py:14
Sparse Core Ops, SparseCore 0:
  10.2 74.4 all-gather.2
